TPU v7x, 32 devices: a whole 2x2x4 slice. The times are simulated.
32 devices in a mesh: sc: 4 (over y, x), rows: 8 (over z, core).
Axes of the slice: x: 2, y: 2, z: 4, core: 2. Of those that a mesh axis runs over, the one named last changes fastest.
Arguments:
- embeddings: bfloat16 [32768, 1024], P(('sc', 'rows')), may hold values from -6 to 6
- labels: int32 [32768, 1], P(('sc', 'rows')), may hold values from 0 to 3; in each aligned block of 1024 rows (0 to 1023, 1024 to 2047, ...) at most 512 rows name the same one
- init_idx: int32 [4, 256], P('sc'), may hold values from 0 to 16383
Outputs:
- assign: bfloat16 [32768, 256], P(('sc', 'rows'))
- centroids: float32 [4, 256, 1024], P('sc')
Inputs may be any that keep to these rules, and one draw needn't show every extreme that they name: `labels`: among the rows of one device (aligned blocks of 1024 rows) no label occurs more than 512 times, and some label occurs exactly 512 times; every label occurs somewhere.
All inputs are finite; a program needn't handle non-finite values.
Results may differ from a plain program's by a relative error of at most 0.0052.
Values may be sent and summed in bfloat16 or wider, within the bound.
A program may use at most 64 MiB of HBM per device.

v0:
```python
import math
import jax
import jax.numpy as jnp
from jax import lax
from jax.sharding import PartitionSpec as P

ITERS = 3
ROUNDS = 3


def carried_in(part, axis, combine, identity):
    place = lax.axis_index(axis)
    gathered = lax.all_gather(part, axis)
    state = jnp.zeros_like(part) + jnp.asarray(identity, part.dtype)

    def one(turn, state):
        return combine(state, lax.dynamic_index_in_dim(gathered, turn, 0, False))

    return lax.fori_loop(0, place, one, state)


def unit_of(rows):
    values = rows.astype(jnp.float32)
    scale = lax.rsqrt(jnp.mean(values * values, axis=1, keepdims=True) + 1e-05) * (
        1.0 / math.sqrt(rows.shape[1])
    )
    return (values * scale).astype(jnp.bfloat16)


def unit_cent(mass):
    return (mass * lax.rsqrt(jnp.sum(mass * mass, axis=1, keepdims=True) + 1e-06)).astype(
        jnp.bfloat16
    )


def on_device(embeddings, labels, init_idx):
    tok = embeddings.shape[0]
    width = embeddings.shape[1]
    groups = lax.axis_size("sc")
    slots = 2 * tok // groups
    label_col = labels[:, 0]
    member = (label_col[:, None] == jnp.arange(groups, dtype=jnp.int32)[None, :]).astype(jnp.int32)
    before_here = jnp.cumsum(member, axis=0) - member
    place = jnp.sum(before_here * member, axis=1)
    counts = jnp.sum(member, axis=0).astype(jnp.float32)
    prefix = carried_in(
        counts, ("sc", "rows"), lambda early, later: early + later, jnp.zeros_like(counts)
    )
    totals = lax.psum(counts, ("sc", "rows"))
    prefix_int = prefix.astype(jnp.int32)
    totals_int = totals.astype(jnp.int32)
    rank = jnp.sum(member * prefix_int[None, :], axis=1) + place
    target = label_col * slots + place
    source = (
        jnp.full((groups * slots,), tok, jnp.int32).at[target].set(jnp.arange(tok, dtype=jnp.int32))
    )
    padded = jnp.concatenate([embeddings, jnp.zeros((1, width), jnp.bfloat16)], axis=0)
    rank_pad = jnp.concatenate([rank, jnp.full((1,), -1, jnp.int32)], axis=0)
    outgoing = padded[source].reshape(groups, slots, width)
    out_rank = rank_pad[source].reshape(groups, slots)
    incoming, in_rank = (
        lax.all_to_all(outgoing, "sc", split_axis=0, concat_axis=0, tiled=True),
        lax.all_to_all(out_rank, "sc", split_axis=0, concat_axis=0, tiled=True),
    )
    incoming = incoming.reshape(groups * slots, width)
    in_rank = in_rank.reshape(groups * slots)
    valid = in_rank >= 0
    members = unit_of(incoming)
    group_here = lax.axis_index("sc")
    count = jnp.sum(jnp.where(jnp.arange(groups, dtype=jnp.int32) == group_here, totals_int, 0))
    wanted = init_idx[0] % count
    picker = (wanted[:, None] == in_rank[None, :]).astype(jnp.bfloat16)
    seeds = jnp.dot(picker, members, preferred_element_type=jnp.float32)
    cent = lax.psum(seeds, "rows").astype(jnp.bfloat16)
    contract_rows = (((0,), (0,)), ((), ()))
    contract_width = (((1,), (1,)), ((), ()))
    for round_index in range(ROUNDS):
        scores = lax.dot_general(members, cent, contract_width, preferred_element_type=jnp.float32)
        plan = jnp.where(valid[:, None], jnp.exp(scores * 10.0), 0.0)
        for step in range(ITERS):
            column = lax.psum(jnp.sum(plan, axis=0), "rows")
            plan = plan / column[None, :]
            row_sum = jnp.sum(plan, axis=1)
            plan = jnp.where(valid[:, None], plan / jnp.where(valid, row_sum, 1.0)[:, None], 0.0)
        plan_b = plan.astype(jnp.bfloat16)
        mass_part = lax.dot_general(
            plan_b, members, contract_rows, preferred_element_type=jnp.float32
        )
        if round_index < ROUNDS - 1:
            mass = lax.psum(mass_part, "rows")
            cent = unit_cent(mass)
        else:
            weight_part = jnp.sum(plan, axis=0)
            mass, weight = lax.psum((mass_part, weight_part), "rows")
            means = mass / weight[:, None]
    plan_out = plan.astype(jnp.bfloat16).reshape(groups, slots, plan.shape[1])
    returned = lax.all_to_all(plan_out, "sc", split_axis=0, concat_axis=0, tiled=True).reshape(
        groups * slots, plan.shape[1]
    )
    assign = returned[target]
    return (assign, means[None])


def solution(mesh):
    return jax.shard_map(
        on_device,
        mesh=mesh,
        in_specs=(P(("sc", "rows"), None), P(("sc", "rows"), None), P("sc", None)),
        out_specs=(P(("sc", "rows"), None), P("sc", None, None)),
        check_vma=False,
    )
```

profile of v0, /device:TPU:0, one launch (start us, length us, event | category | flops | bytes accessed | tf_op | source)
XLA Modules:
  0.0 568.7 jit_solution(1118507430221130394)
XLA Ops:
  8.1 42.0 %all-reduce.2 = (f32[128]{0:T(128)S(1)}, f32[4]{0:T(128)S(1)}) all-reduce(f32[128]{0:T(128)S(1)} %convert_dynamic-update-slice_fusion, f32[4]{0:T(128)S(1)} %convert_element_type.59), channel_id=2, replica_groups=mesh['sc'=4,'rows'=8] {'sc','rows'}, use_global_device_ids=true, to_apply=%add.1 | all-reduce | flops 132 | bytes 1056
  54.0 4.3 scatter_custom_fusion
  58.4 20.6 %gather_fusion = s32[2048]{0:T(1024)} fusion(s32[1025]{0:T(1024)S(1)} %pad_add_fusion, s32[2048]{0:T(1024)S(1)} %fusion.27), kind=kCustom, calls=%fused_computation | custom fusion | bytes 24576 | tf_op jit(solution)/shard_map/gather | solution.py:60
  78.9 4.4 all-to-all-start
  85.1 9.7 %gather_fusion.1 = bf16[2048,1024]{1,0:T(8,128)(2,1)} fusion(bf16[1025,1024]{1,0:T(8,128)(2,1)S(1)} %concatenate.7, s32[2048]{0:T(1024)S(1)} %fusion.27), kind=kCustom, calls=%fused_computation.1 | custom fusion | bytes 8396800 | tf_op jit(solution)/shard_map/gather | solution.py:59
  94.8 5.0 all-to-all-start.1
  101.9 44.5 %all-to-all-done.1 = bf16[4,512,1024]{2,1,0:T(8,128)(2,1)} async-done(((bf16[4,512,1024]{2,1,0:T(8,128)(2,1)}), bf16[4,512,1024]{2,1,0:T(8,128)(2,1)}, u32[]{:S(2)}, u32[]{:S(2)}) %all-to-all-start.1) | async-done | bytes 4194336 | tf_op jit(solution)/shard_map/all_to_all | solution.py:62
  155.8 57.9 %all-reduce.13 = bf16[256,1024]{1,0:T(8,128)(2,1)S(1)} all-reduce(f32[256,1024]{1,0:T(8,128)S(1)} %fusion.7), channel_id=1, replica_groups=mesh['sc'=4,'rows'=8] {'rows'}, use_global_device_ids=true, to_apply=%region_11.12 | all-reduce | flops 262144 | bytes 1572864 | tf_op jit(solution)/shard_map/psum | solution.py:74
  216.8 15.1 %psum.107 = f32[256]{0:T(256)S(1)} all-reduce(f32[256]{0:T(256)S(1)} %get-tuple-element.52), channel_id=1, replica_groups=mesh['sc'=4,'rows'=8] {'rows'}, use_global_device_ids=true, to_apply=%region_13.14 | all-reduce | flops 256 | bytes 2048 | tf_op jit(solution)/shard_map/psum | solution.py:81
  234.3 13.6 %psum.108 = f32[256]{0:T(256)S(1)} all-reduce(f32[256]{0:T(256)S(1)} %get-tuple-element.48), channel_id=1, replica_groups=mesh['sc'=4,'rows'=8] {'rows'}, use_global_device_ids=true, to_apply=%region_16.17 | all-reduce | flops 256 | bytes 2048 | tf_op jit(solution)/shard_map/psum | solution.py:81
  250.0 13.7 %psum.109 = f32[256]{0:T(256)S(1)} all-reduce(f32[256]{0:T(256)S(1)} %get-tuple-element.46), channel_id=1, replica_groups=mesh['sc'=4,'rows'=8] {'rows'}, use_global_device_ids=true, to_apply=%region_19.20 | all-reduce | flops 256 | bytes 2048 | tf_op jit(solution)/shard_map/psum | solution.py:81
  265.7 4.9 fusion.9
  270.9 56.0 %all-reduce.8.cloned.1.call-done = f32[256,1024]{1,0:T(8,128)} async-done(((f32[256,1024]{1,0:T(8,128)}), f32[256,1024]{1,0:T(8,128)}) %all-reduce.8.cloned.1.call-update) | async-done | bytes 1048592 | tf_op jit(solution)/shard_map/psum | solution.py:90
  331.8 13.6 %psum.111 = f32[256]{0:T(256)S(1)} all-reduce(f32[256]{0:T(256)S(1)} %get-tuple-element.54), channel_id=1, replica_groups=mesh['sc'=4,'rows'=8] {'rows'}, use_global_device_ids=true, to_apply=%region_24.25 | all-reduce | flops 256 | bytes 2048 | tf_op jit(solution)/shard_map/psum | solution.py:81
  347.7 13.6 %psum.112 = f32[256]{0:T(256)S(1)} all-reduce(f32[256]{0:T(256)S(1)} %get-tuple-element.44), channel_id=1, replica_groups=mesh['sc'=4,'rows'=8] {'rows'}, use_global_device_ids=true, to_apply=%region_27.28 | all-reduce | flops 256 | bytes 2048 | tf_op jit(solution)/shard_map/psum | solution.py:81
  363.4 13.7 %psum.113 = f32[256]{0:T(256)S(1)} all-reduce(f32[256]{0:T(256)S(1)} %get-tuple-element.42), channel_id=1, replica_groups=mesh['sc'=4,'rows'=8] {'rows'}, use_global_device_ids=true, to_apply=%region_30.31 | all-reduce | flops 256 | bytes 2048 | tf_op jit(solution)/shard_map/psum | solution.py:81
  379.1 4.9 fusion.10
  384.1 57.0 %all-reduce.10.cloned.1.call-done = f32[256,1024]{1,0:T(8,128)} async-done(((f32[256,1024]{1,0:T(8,128)}), f32[256,1024]{1,0:T(8,128)}) %all-reduce.10.cloned.1.call-update) | async-done | bytes 1048592 | tf_op jit(solution)/shard_map/psum | solution.py:90
  446.1 13.6 %psum.115 = f32[256]{0:T(256)S(1)} all-reduce(f32[256]{0:T(256)S(1)} %get-tuple-element.56), channel_id=1, replica_groups=mesh['sc'=4,'rows'=8] {'rows'}, use_global_device_ids=true, to_apply=%region_35.36 | all-reduce | flops 256 | bytes 2048 | tf_op jit(solution)/shard_map/psum | solution.py:81
  462.1 13.6 %psum.116 = f32[256]{0:T(256)S(1)} all-reduce(f32[256]{0:T(256)S(1)} %get-tuple-element.40), channel_id=1, replica_groups=mesh['sc'=4,'rows'=8] {'rows'}, use_global_device_ids=true, to_apply=%region_38.39 | all-reduce | flops 256 | bytes 2048 | tf_op jit(solution)/shard_map/psum | solution.py:81
  478.0 13.6 %psum.117 = f32[256]{0:T(256)S(1)} all-reduce(f32[256]{0:T(256)S(1)} %get-tuple-element.38), channel_id=1, replica_groups=mesh['sc'=4,'rows'=8] {'rows'}, use_global_device_ids=true, to_apply=%region_41.42 | all-reduce | flops 256 | bytes 2048 | tf_op jit(solution)/shard_map/psum | solution.py:81
  501.3 13.9 %psum.119 = f32[256]{0:T(256)S(1)} all-reduce(f32[256]{0:T(256)S(1)} %get-tuple-element.50), channel_id=1, replica_groups=mesh['sc'=4,'rows'=8] {'rows'}, use_global_device_ids=true, to_apply=%region_45.46 | all-reduce | flops 256 | bytes 2048 | tf_op jit(solution)/shard_map/psum | solution.py:94
  515.2 39.6 %all-reduce.12.cloned.1.call-done = f32[256,1024]{1,0:T(8,128)} async-done(((f32[256,1024]{1,0:T(8,128)}), f32[256,1024]{1,0:T(8,128)}) %all-reduce.12.cloned.1.call-update) | async-done | bytes 1048592 | tf_op jit(solution)/shard_map/psum | solution.py:94
  557.2 5.0 gather_fusion.2
  (91 shorter events, 59.4 us)
Async XLA Ops:
  78.9 15.9 %all-to-all-start = ((s32[4,1,512]{2,1,0:T(1,128)}), s32[4,1,512]{2,1,0:T(1,128)S(1)}, u32[]{:S(2)}, u32[]{:S(2)}) async-start(s32[4,1,512]{2,1,0:T(1,128)} %bitcast.6), calls=%async_computation | async-start | bytes 16384 | tf_op jit(solution)/shard_map/all_to_all | solution.py:63
  94.8 7.0 %copy-start.8 = (s32[1,256]{1,0:T(1,128)S(1)}, s32[1,256]{1,0:T(1,128)}, u32[]{:S(2)}) copy-start(s32[1,256]{1,0:T(1,128)} %param.7) | copy-start | bytes 3076
  94.8 51.7 %all-to-all-start.1 = ((bf16[4,512,1024]{2,1,0:T(8,128)(2,1)}), bf16[4,512,1024]{2,1,0:T(8,128)(2,1)}, u32[]{:S(2)}, u32[]{:S(2)}) async-start(bf16[4,512,1024]{2,1,0:T(8,128)(2,1)} %bitcast.45), calls=%async_computation.1 | async-start | bytes 8388608 | tf_op jit(solution)/shard_map/all_to_all | solution.py:62
  99.8 227.1 %all-reduce.8.cloned.1.call-start = ((), (), s32[]{:S(2)}) async-start(), calls=%async_computation.3 | async-start | bytes 2097152 | tf_op jit(solution)/shard_map/psum | solution.py:90
  152.5 1.9 copy-start.6
  216.8 15.5 %copy-start.3 = (f32[2048,256]{1,0:T(8,128)}, f32[2048,256]{1,0:T(8,128)S(1)}, u32[]{:S(2)}) copy-start(f32[2048,256]{1,0:T(8,128)S(1)} %get-tuple-element.53) | copy-start | bytes 6291460
  250.0 15.7 %copy-start.4 = (f32[2048,256]{1,0:T(8,128)S(1)}, f32[2048,256]{1,0:T(8,128)}, u32[]{:S(2)}) copy-start(f32[2048,256]{1,0:T(8,128)} %get-tuple-element.47) | copy-start | bytes 6291460
  270.6 170.5 %all-reduce.10.cloned.1.call-start = ((), (), s32[]{:S(2)}) async-start(), calls=%async_computation.4 | async-start | bytes 2097152 | tf_op jit(solution)/shard_map/psum | solution.py:90
  331.8 14.0 %copy-start.1 = (f32[2048,256]{1,0:T(8,128)}, f32[2048,256]{1,0:T(8,128)S(1)}, u32[]{:S(2)}) copy-start(f32[2048,256]{1,0:T(8,128)S(1)} %get-tuple-element.55) | copy-start | bytes 6291460
  363.4 15.7 %copy-start.5 = (f32[2048,256]{1,0:T(8,128)S(1)}, f32[2048,256]{1,0:T(8,128)}, u32[]{:S(2)}) copy-start(f32[2048,256]{1,0:T(8,128)} %get-tuple-element.43) | copy-start | bytes 6291460
  384.1 170.8 %all-reduce.12.cloned.1.call-start = ((), (), s32[]{:S(2)}) async-start(), calls=%async_computation.5 | async-start | bytes 2097152 | tf_op jit(solution)/shard_map/psum | solution.py:94
  446.1 14.0 %copy-start.2 = (f32[2048,256]{1,0:T(8,128)}, f32[2048,256]{1,0:T(8,128)S(1)}, u32[]{:S(2)}) copy-start(f32[2048,256]{1,0:T(8,128)S(1)} %get-tuple-element.57) | copy-start | bytes 6291460
  462.1 14.0 %copy-start = (f32[2048,256]{1,0:T(8,128)}, f32[2048,256]{1,0:T(8,128)S(1)}, u32[]{:S(2)}) copy-start(f32[2048,256]{1,0:T(8,128)S(1)} %get-tuple-element.41) | copy-start | bytes 6291460
  491.6 2.6 copy-start.7
  497.7 59.5 %all-to-all-start.2 = ((bf16[4,512,256]{2,1,0:T(8,128)(2,1)}), bf16[4,512,256]{2,1,0:T(8,128)(2,1)S(1)}, u32[]{:S(2)}, u32[]{:S(2)}) async-start(bf16[4,512,256]{2,1,0:T(8,128)(2,1)} %bitcast.11), calls=%async_computation.2 | async-start | bytes 2097152 | tf_op jit(solution)/shard_map/all_to_all | solution.py:97
Sparse Core Ops, SparseCore 0:
  270.8 56.0 all-reduce.7
  384.2 56.9 all-reduce.9
  497.8 56.9 all-reduce.11
where the time goes:
time: 570 us; the launch traced here: 569 us
  blocking collectives  238 us (42%)
  waiting for transfers between devices  197 us (35%)
  local copies, waits for them, and re-layouts  44.2 us (8%)
  other arithmetic  35.6 us (6%)
  matrix products  25 us (4%)
  between operations  15.5 us (3%)
  starting transfers between devices  13.4 us (2%)
    psum x9, blocking collectives, on_device(): column = lax.psum(jnp.sum(plan, axis=0), 'rows')  124 us
    psum x2, waiting for transfers between devices, on_device(): mass = lax.psum(mass_part, 'rows')  113 us
    psum x1, blocking collectives, on_device(): cent = lax.psum(seeds, 'rows').astype(jnp.bfloat16)  57.9 us
    all_to_all x1, waiting for transfers between devices, on_device(): lax.all_to_all(outgoing, 'sc', split_axis=0, concat_axis=0, tiled=True)  44.5 us
    unnamed x1, blocking collectives  42 us
    psum x1, waiting for transfers between devices, on_device(): mass, weight = lax.psum((mass_part, weight_part), 'rows')  39.6 us
    gather x1, local copies, waits for them, and re-layouts, on_device(): out_rank = rank_pad[source].reshape(groups, slots)  20.6 us
    psum x1, blocking collectives, on_device(): mass, weight = lax.psum((mass_part, weight_part), 'rows')  13.9 us
  transfers between devices with their start and end apart: 6, of which 4 were waited for; matrix products, arithmetic and copies ran while one was open for 3% of the time, Pallas kernels for 0%

commit v1 on v0

--- a/solution.py
+++ b/solution.py
@@ -78,7 +78,7 @@
         scores = lax.dot_general(members, cent, contract_width, preferred_element_type=jnp.float32)
         plan = jnp.where(valid[:, None], jnp.exp(scores * 10.0), 0.0)
         for step in range(ITERS):
-            column = lax.psum(jnp.sum(plan, axis=0), "rows")
+            column = jnp.sum(lax.all_gather(jnp.sum(plan, axis=0), "rows"), axis=0)
             plan = plan / column[None, :]
             row_sum = jnp.sum(plan, axis=1)
             plan = jnp.where(valid[:, None], plan / jnp.where(valid, row_sum, 1.0)[:, None], 0.0)

time: 570 us -> 531 us (0.932)
  blocking collectives: 238 us -> 199 us
    psum x9 -> x0, blocking collectives: 124 us -> none  [on_device(): column = lax.psum(jnp.sum(plan, axis=0), 'rows')]
    all_gather x0 -> x9, blocking collectives: none -> 84.8 us  [on_device(): column = jnp.sum(lax.all_gather(jnp.sum(plan, axis=0), 'rows'), axis=0)]
    reduce_sum x6 -> x15, other arithmetic: 11.3 us -> 11.6 us  [on_device(): column = jnp.sum(lax.all_gather(jnp.sum(plan, axis=0), 'rows'), axis=0)]
where the time goes in v1:
time: 531 us; the launch traced here: 530 us
  blocking collectives  199 us (37%)
  waiting for transfers between devices  197 us (37%)
  local copies, waits for them, and re-layouts  44.2 us (8%)
  other arithmetic  35.8 us (7%)
  matrix products  25 us (5%)
  between operations  15.5 us (3%)
  starting transfers between devices  13.4 us (3%)
    psum x2, waiting for transfers between devices, on_device(): mass = lax.psum(mass_part, 'rows')  113 us
    all_gather x9, blocking collectives, on_device(): column = jnp.sum(lax.all_gather(jnp.sum(plan, axis=0), 'rows'), axis=0)  84.8 us
    psum x1, blocking collectives, on_device(): cent = lax.psum(seeds, 'rows').astype(jnp.bfloat16)  57.9 us
    all_to_all x1, waiting for transfers between devices, on_device(): lax.all_to_all(outgoing, 'sc', split_axis=0, concat_axis=0, tiled=True)  44.5 us
    unnamed x1, blocking collectives  42 us
    psum x1, waiting for transfers between devices, on_device(): mass, weight = lax.psum((mass_part, weight_part), 'rows')  39.3 us
    gather x1, local copies, waits for them, and re-layouts, on_device(): out_rank = rank_pad[source].reshape(groups, slots)  20.6 us
    psum x1, blocking collectives, on_device(): mass, weight = lax.psum((mass_part, weight_part), 'rows')  14.3 us
  transfers between devices with their start and end apart: 6, of which 4 were waited for; matrix products, arithmetic and copies ran while one was open for 3% of the time, Pallas kernels for 0%

profile of v1, /device:TPU:0, one launch (start us, length us, event | category | flops | bytes accessed | tf_op | source)
XLA Modules:
  0.0 530.2 jit_solution(16481196642982618985)
XLA Ops:
  8.1 42.0 %all-reduce.2 = (f32[128]{0:T(128)S(1)}, f32[4]{0:T(128)S(1)}) all-reduce(f32[128]{0:T(128)S(1)} %convert_dynamic-update-slice_fusion, f32[4]{0:T(128)S(1)} %convert_element_type.59), channel_id=2, replica_groups=mesh['sc'=4,'rows'=8] {'sc','rows'}, use_global_device_ids=true, to_apply=%add.1 | all-reduce | flops 132 | bytes 1056
  54.0 4.3 scatter_custom_fusion
  58.4 20.6 %gather_fusion = s32[2048]{0:T(1024)} fusion(s32[1025]{0:T(1024)S(1)} %pad_add_fusion, s32[2048]{0:T(1024)S(1)} %fusion.27), kind=kCustom, calls=%fused_computation | custom fusion | bytes 24576 | tf_op jit(solution)/shard_map/gather | solution.py:60
  78.9 4.4 all-to-all-start
  85.1 9.7 %gather_fusion.1 = bf16[2048,1024]{1,0:T(8,128)(2,1)} fusion(bf16[1025,1024]{1,0:T(8,128)(2,1)S(1)} %concatenate.7, s32[2048]{0:T(1024)S(1)} %fusion.27), kind=kCustom, calls=%fused_computation.1 | custom fusion | bytes 8396800 | tf_op jit(solution)/shard_map/gather | solution.py:59
  94.8 5.0 all-to-all-start.1
  101.9 44.5 %all-to-all-done.1 = bf16[4,512,1024]{2,1,0:T(8,128)(2,1)} async-done(((bf16[4,512,1024]{2,1,0:T(8,128)(2,1)}), bf16[4,512,1024]{2,1,0:T(8,128)(2,1)}, u32[]{:S(2)}, u32[]{:S(2)}) %all-to-all-start.1) | async-done | bytes 4194336 | tf_op jit(solution)/shard_map/all_to_all | solution.py:62
  155.8 57.9 %all-reduce.13 = bf16[256,1024]{1,0:T(8,128)(2,1)S(1)} all-reduce(f32[256,1024]{1,0:T(8,128)S(1)} %fusion.7), channel_id=1, replica_groups=mesh['sc'=4,'rows'=8] {'rows'}, use_global_device_ids=true, to_apply=%region_11.12 | all-reduce | flops 262144 | bytes 1572864 | tf_op jit(solution)/shard_map/psum | solution.py:74
  216.8 8.4 %all-gather.10 = f32[8,1,256]{2,1,0:T(1,128)S(1)} all-gather(f32[1,1,256]{2,1,0:T(1,128)S(1)} %bitcast.83), channel_id=3, replica_groups=mesh['sc'=4,'rows'=8] {'rows'}, dimensions={0}, use_global_device_ids=true | all-gather | bytes 9216 | tf_op jit(solution)/shard_map/all_gather | solution.py:81
  227.6 10.4 %all-gather.11 = f32[8,1,256]{2,1,0:T(1,128)S(1)} all-gather(f32[1,1,256]{2,1,0:T(1,128)S(1)} %bitcast.74), channel_id=4, replica_groups=mesh['sc'=4,'rows'=8] {'rows'}, dimensions={0}, use_global_device_ids=true | all-gather | bytes 9216 | tf_op jit(solution)/shard_map/all_gather | solution.py:81
  240.2 8.8 %all-gather.12 = f32[8,1,256]{2,1,0:T(1,128)S(1)} all-gather(f32[1,1,256]{2,1,0:T(1,128)S(1)} %bitcast.75), channel_id=5, replica_groups=mesh['sc'=4,'rows'=8] {'rows'}, dimensions={0}, use_global_device_ids=true | all-gather | bytes 9216 | tf_op jit(solution)/shard_map/all_gather | solution.py:81
  251.0 5.0 fusion.9
  256.2 56.2 %all-reduce.8.cloned.1.call-done = f32[256,1024]{1,0:T(8,128)} async-done(((f32[256,1024]{1,0:T(8,128)}), f32[256,1024]{1,0:T(8,128)}) %all-reduce.8.cloned.1.call-update) | async-done | bytes 1048592 | tf_op jit(solution)/shard_map/psum | solution.py:90
  317.4 9.7 %all-gather.13 = f32[8,1,256]{2,1,0:T(1,128)S(1)} all-gather(f32[1,1,256]{2,1,0:T(1,128)S(1)} %bitcast.81), channel_id=6, replica_groups=mesh['sc'=4,'rows'=8] {'rows'}, dimensions={0}, use_global_device_ids=true | all-gather | bytes 9216 | tf_op jit(solution)/shard_map/all_gather | solution.py:81
  329.5 9.1 %all-gather.14 = f32[8,1,256]{2,1,0:T(1,128)S(1)} all-gather(f32[1,1,256]{2,1,0:T(1,128)S(1)} %bitcast.76), channel_id=7, replica_groups=mesh['sc'=4,'rows'=8] {'rows'}, dimensions={0}, use_global_device_ids=true | all-gather | bytes 9216 | tf_op jit(solution)/shard_map/all_gather | solution.py:81
  340.7 9.8 %all-gather.15 = f32[8,1,256]{2,1,0:T(1,128)S(1)} all-gather(f32[1,1,256]{2,1,0:T(1,128)S(1)} %bitcast.77), channel_id=8, replica_groups=mesh['sc'=4,'rows'=8] {'rows'}, dimensions={0}, use_global_device_ids=true | all-gather | bytes 9216 | tf_op jit(solution)/shard_map/all_gather | solution.py:81
  352.5 4.9 fusion.10
  357.5 57.3 %all-reduce.10.cloned.1.call-done = f32[256,1024]{1,0:T(8,128)} async-done(((f32[256,1024]{1,0:T(8,128)}), f32[256,1024]{1,0:T(8,128)}) %all-reduce.10.cloned.1.call-update) | async-done | bytes 1048592 | tf_op jit(solution)/shard_map/psum | solution.py:90
  419.8 9.7 %all-gather.16 = f32[8,1,256]{2,1,0:T(1,128)S(1)} all-gather(f32[1,1,256]{2,1,0:T(1,128)S(1)} %bitcast.82), channel_id=9, replica_groups=mesh['sc'=4,'rows'=8] {'rows'}, dimensions={0}, use_global_device_ids=true | all-gather | bytes 9216 | tf_op jit(solution)/shard_map/all_gather | solution.py:81
  431.9 9.1 %all-gather.17 = f32[8,1,256]{2,1,0:T(1,128)S(1)} all-gather(f32[1,1,256]{2,1,0:T(1,128)S(1)} %bitcast.78), channel_id=10, replica_groups=mesh['sc'=4,'rows'=8] {'rows'}, dimensions={0}, use_global_device_ids=true | all-gather | bytes 9216 | tf_op jit(solution)/shard_map/all_gather | solution.py:81
  443.3 9.7 %all-gather.18 = f32[8,1,256]{2,1,0:T(1,128)S(1)} all-gather(f32[1,1,256]{2,1,0:T(1,128)S(1)} %bitcast.79), channel_id=11, replica_groups=mesh['sc'=4,'rows'=8] {'rows'}, dimensions={0}, use_global_device_ids=true | all-gather | bytes 9216 | tf_op jit(solution)/shard_map/all_gather | solution.py:81
  462.8 14.3 %psum.47 = f32[256]{0:T(256)S(1)} all-reduce(f32[256]{0:T(256)S(1)} %get-tuple-element.50), channel_id=1, replica_groups=mesh['sc'=4,'rows'=8] {'rows'}, use_global_device_ids=true, to_apply=%region_45.46 | all-reduce | flops 256 | bytes 2048 | tf_op jit(solution)/shard_map/psum | solution.py:94
  477.1 39.3 %all-reduce.12.cloned.1.call-done = f32[256,1024]{1,0:T(8,128)} async-done(((f32[256,1024]{1,0:T(8,128)}), f32[256,1024]{1,0:T(8,128)}) %all-reduce.12.cloned.1.call-update) | async-done | bytes 1048592 | tf_op jit(solution)/shard_map/psum | solution.py:94
  518.7 5.0 gather_fusion.2
  (100 shorter events, 59.7 us)
Async XLA Ops:
  78.9 15.9 %all-to-all-start = ((s32[4,1,512]{2,1,0:T(1,128)}), s32[4,1,512]{2,1,0:T(1,128)S(1)}, u32[]{:S(2)}, u32[]{:S(2)}) async-start(s32[4,1,512]{2,1,0:T(1,128)} %bitcast.6), calls=%async_computation | async-start | bytes 16384 | tf_op jit(solution)/shard_map/all_to_all | solution.py:63
  94.8 7.0 %copy-start.8 = (s32[1,256]{1,0:T(1,128)S(1)}, s32[1,256]{1,0:T(1,128)}, u32[]{:S(2)}) copy-start(s32[1,256]{1,0:T(1,128)} %param.7) | copy-start | bytes 3076
  94.8 51.7 %all-to-all-start.1 = ((bf16[4,512,1024]{2,1,0:T(8,128)(2,1)}), bf16[4,512,1024]{2,1,0:T(8,128)(2,1)}, u32[]{:S(2)}, u32[]{:S(2)}) async-start(bf16[4,512,1024]{2,1,0:T(8,128)(2,1)} %bitcast.54), calls=%async_computation.1 | async-start | bytes 8388608 | tf_op jit(solution)/shard_map/all_to_all | solution.py:62
  99.8 212.6 %all-reduce.8.cloned.1.call-start = ((), (), s32[]{:S(2)}) async-start(), calls=%async_computation.3 | async-start | bytes 2097152 | tf_op jit(solution)/shard_map/psum | solution.py:90
  152.5 1.9 copy-start.6
  216.8 8.8 %copy-start.3 = (f32[2048,256]{1,0:T(8,128)}, f32[2048,256]{1,0:T(8,128)S(1)}, u32[]{:S(2)}) copy-start(f32[2048,256]{1,0:T(8,128)S(1)} %get-tuple-element.53) | copy-start | bytes 6291460
  240.2 10.8 %copy-start.4 = (f32[2048,256]{1,0:T(8,128)S(1)}, f32[2048,256]{1,0:T(8,128)}, u32[]{:S(2)}) copy-start(f32[2048,256]{1,0:T(8,128)} %get-tuple-element.47) | copy-start | bytes 6291460
  256.0 158.8 %all-reduce.10.cloned.1.call-start = ((), (), s32[]{:S(2)}) async-start(), calls=%async_computation.4 | async-start | bytes 2097152 | tf_op jit(solution)/shard_map/psum | solution.py:90
  317.4 10.1 %copy-start.1 = (f32[2048,256]{1,0:T(8,128)}, f32[2048,256]{1,0:T(8,128)S(1)}, u32[]{:S(2)}) copy-start(f32[2048,256]{1,0:T(8,128)S(1)} %get-tuple-element.55) | copy-start | bytes 6291460
  340.7 11.8 %copy-start.5 = (f32[2048,256]{1,0:T(8,128)S(1)}, f32[2048,256]{1,0:T(8,128)}, u32[]{:S(2)}) copy-start(f32[2048,256]{1,0:T(8,128)} %get-tuple-element.43) | copy-start | bytes 6291460
  357.5 158.9 %all-reduce.12.cloned.1.call-start = ((), (), s32[]{:S(2)}) async-start(), calls=%async_computation.5 | async-start | bytes 2097152 | tf_op jit(solution)/shard_map/psum | solution.py:94
  419.7 10.1 %copy-start.2 = (f32[2048,256]{1,0:T(8,128)}, f32[2048,256]{1,0:T(8,128)S(1)}, u32[]{:S(2)}) copy-start(f32[2048,256]{1,0:T(8,128)S(1)} %get-tuple-element.57) | copy-start | bytes 6291460
  431.9 9.5 %copy-start = (f32[2048,256]{1,0:T(8,128)}, f32[2048,256]{1,0:T(8,128)S(1)}, u32[]{:S(2)}) copy-start(f32[2048,256]{1,0:T(8,128)S(1)} %get-tuple-element.41) | copy-start | bytes 6291460
  453.1 2.6 copy-start.7
  459.2 59.6 %all-to-all-start.2 = ((bf16[4,512,256]{2,1,0:T(8,128)(2,1)}), bf16[4,512,256]{2,1,0:T(8,128)(2,1)S(1)}, u32[]{:S(2)}, u32[]{:S(2)}) async-start(bf16[4,512,256]{2,1,0:T(8,128)(2,1)} %bitcast.20), calls=%async_computation.2 | async-start | bytes 2097152 | tf_op jit(solution)/shard_map/all_to_all | solution.py:97
Sparse Core Ops, SparseCore 0:
  256.1 56.2 all-reduce.7
  357.6 57.1 all-reduce.9
  459.3 57.0 all-reduce.11
